TPU v7x, 256 devices: a whole 4x4x8 slice. The times are simulated.
256 devices in a mesh: blk: 16 (over y, x_lo, core), grp: 16 (over z, x_hi).
Axes of the slice: x: 4 (x_hi: 2, x_lo: 2; x = x_hi * 2 + x_lo), y: 4, z: 8, core: 2. Of those that a mesh axis runs over, the one named last changes fastest.
Arguments:
- source_rows: float32 [16, 16, 400, 768], P('blk', 'grp'), may hold values from -2.4 to 2.4
- source_state: float32 [16, 16, 768], P('blk', 'grp'), may hold values from 0.05 to 1
- target_rows: float32 [16, 16, 400, 512], P('blk', 'grp'), may hold values from -12.5 to 12.5
- destination_state: float32 [16, 16, 512], P('blk', 'grp'), may hold values from 0.05 to 1
- positives: int32 [4, 16, 16, 768], P(None, 'blk', 'grp'), may hold values from 0 to 511
- relation_ids: int32 [4, 16, 16], P(None, 'blk', 'grp'), may hold values from 0 to 1
- relations: float32 [2, 400, 400], replicated, may hold values from -0.36 to 1.36
Outputs:
- source_out: float32 [16, 16, 400, 768], P('blk', 'grp')
- source_state_out: float32 [16, 16, 768], P('blk', 'grp')
- target_out: float32 [16, 16, 400, 512], P('blk', 'grp')
- target_state_out: float32 [16, 16, 512], P('blk', 'grp')
- relations_out: float32 [2, 400, 400], replicated
- operator_grads: float32 [2, 2, 400, 400], replicated
All inputs are finite; a program needn't handle non-finite values.
Results may differ from a plain program's by a relative error of at most 0.0003.
Values sent between devices are 32-bit elements; how exact they have to be, the bound alone decides.
A program may use at most 64 MiB of HBM per device.

v0:
```python
import functools
import math

import jax
import jax.numpy as jnp
from jax import lax
from jax.experimental import pallas as pl
from jax.experimental.pallas import tpu as pltpu
from jax.sharding import PartitionSpec as P

entity_rate = 0.1
operator_rate = 0.01
grad_gain = 6.0

f32, bf16 = jnp.float32, jnp.bfloat16
MESH = pl.DeviceIdType.MESH

W = 400
S = 768
D = 512
C = 256
STEPS = 4
NX, NY, NZ = 4, 4, 8
MAIN, TAIL, TILES = 150, 8, 320
HALF, P1, P2, P3 = TILES // 2, TILES // 8, TILES // 32, 2
N_EX, N_1, N_2, N_3, N_4, N_5, N_6, N_7, N_ALL = 0, 1, 4, 7, 14, 21, 24, 27, 31


def dot(a, b, ca, cb):
    return lax.dot_general(a, b, (((ca,), (cb,)), ((), ())), preferred_element_type=f32)


def split(v):
    high = v.astype(bf16)
    return high, (v - high.astype(f32)).astype(bf16)


def dot3(ah, al, bh, bl, ca, cb):
    return dot(ah, bh, ca, cb) + (dot(ah, bl, ca, cb) + dot(al, bh, ca, cb))


def dot3_rows(ah, al, bh, bl):
    left = jnp.concatenate([ah, ah, al], axis=0)
    right = jnp.concatenate([bh, bl, bh], axis=0)
    return dot(left, right, 0, 0)


def adagrad(values, state, gradient):
    state_new = state + jnp.sum(gradient * gradient, axis=0, keepdims=True) * (1.0 / W)
    return values - gradient * (entity_rate / jnp.sqrt(state_new)), state_new


def kernel(
    gradient_scale,
    x_in,
    xst_in,
    y_in,
    yst_in,
    pos,
    rid,
    rel_in,
    x,
    xst,
    y_out,
    yst_out,
    rel,
    og_out,
    yin,
    ysend,
    xh,
    xl,
    yh,
    yl,
    qh,
    ql,
    sc,
    sh,
    sl,
    gh,
    gl,
    rh,
    rl,
    acc,
    rx,
    r1,
    b1,
    r2,
    b2,
    r3,
    g3,
    g2,
    gall,
    y_ssem,
    y_rsem,
    ssem,
    rsem,
):
    blk, grp = lax.axis_index("blk"), lax.axis_index("grp")
    core = blk % 2
    my_y = blk // 4
    my_x = (grp % 2) * 2 + (blk // 2) % 2
    my_z = grp // 2
    first = my_x * (1 - core) + my_y * core
    second = my_y * (1 - core) + my_x * core

    def at(px, py, pz, pc):
        return ((py * 2 + px % 2) * 2 + pc, pz * 2 + px // 2)

    def first_peer(p):
        return at(p * (1 - core) + my_x * core, p * core + my_y * (1 - core), my_z, core)

    def second_peer(p):
        return at(p * core + my_x * (1 - core), p * (1 - core) + my_y * core, my_z, core)

    def z_peer(p):
        return at(my_x, my_y, p, core)

    other = at(my_x, my_y, my_z, 1 - core)
    behind = ((blk + 1) % 16, grp)
    far = ((blk + 15 + 2 * core) % 16, grp)

    barrier = pltpu.get_barrier_semaphore()
    peers = [other, far]
    peers += [first_peer((first + j) % 4) for j in range(1, 4)]
    peers += [second_peer((second + j) % 4) for j in range(1, 4)]
    peers += [z_peer((my_z + j) % NZ) for j in range(1, NZ)]
    for peer in peers:
        pl.semaphore_signal(barrier, inc=1, device_id=peer, device_id_type=MESH)

    x[...] = x_in[...]
    xst[...] = xst_in[...]
    rel[...] = rel_in[...]
    xh[...], xl[...] = split(x_in[...])
    rh[...], rl[...] = split(rel_in[...])
    for c in range(2):
        yin[0, c, :W] = y_in[:, c * C : (c + 1) * C]
        yin[0, c, W:] = jnp.broadcast_to(yst_in[:, c * C : (c + 1) * C], (8, C))
    gh[W:] = jnp.zeros((D - W, S), bf16)
    gl[W:] = jnp.zeros((D - W, S), bf16)
    acc[2 * MAIN :] = jnp.zeros((TILES - 2 * MAIN, 8, 128), f32)
    b2[P2:] = jnp.zeros((P3 * NZ - P2, 8, 128), f32)

    pl.semaphore_wait(barrier, len(peers))

    def queries(k):
        r = rid[k]
        qh[...], ql[...] = split(dot3_rows(rh[r], rl[r], xh[...], xl[...]))

    def scores(k, arrived):
        for c in range(2):
            if arrived is not None:
                arrived[c].wait_recv()
            high, low = split(yin[k, c, :W])
            yh[:, c * C : (c + 1) * C] = high
            yl[:, c * C : (c + 1) * C] = low
            sc[c * C : (c + 1) * C] = dot3_rows(high, low, qh[...], ql[...])
        for n in range(3):
            part = slice(n * 256, (n + 1) * 256)
            s = sc[:, part]
            e = jnp.exp(s - jnp.max(s, axis=0, keepdims=True))
            chance = e * (1.0 / jnp.sum(e, axis=0, keepdims=True))
            rows = lax.broadcasted_iota(jnp.int32, (D, 256), 0)
            onehot = (rows == pos[k, :, part]).astype(f32)
            sh[:, part], sl[:, part] = split(chance - onehot)

    def new_targets(k, c):
        part = slice(c * C, (c + 1) * C)
        grad = dot3(qh[...], ql[...], sh[part], sl[part], 1, 1)
        rows, state = adagrad(yin[k, c, :W], yin[k, c, W : W + 1], grad)
        ysend[k, c, :W] = rows
        ysend[k, c, W:] = jnp.broadcast_to(state, (8, C))

    def send_targets(k, c):
        copy = pltpu.make_async_remote_copy(
            src_ref=ysend.at[k, c],
            dst_ref=yin.at[k + 1, c],
            send_sem=y_ssem.at[k, c],
            recv_sem=y_rsem.at[k, c],
            device_id=behind,
            device_id_type=MESH,
        )
        copy.start()
        return copy

    def query_grad():
        gh[:W], gl[:W] = split(dot3(yh[...], yl[...], sh[...], sl[...], 1, 0))

    def operator_grad(k, add):
        og = dot3(xh[...], xl[...], gh[...], gl[...], 1, 1)
        tail = og[:, 384:].T[:16]
        for r in range(2):
            mine = (rid[k] == r).astype(f32)
            for c in range(3):
                at_ = pl.ds(r * MAIN + c * 50, 50)
                part = mine * og[:, c * 128 : (c + 1) * 128].reshape(50, 8, 128)
                acc[at_] = acc[at_] + part if add else part
            for i in range(2):
                for c in range(4):
                    n = 128 if c < 3 else 16
                    t = 2 * MAIN + r * TAIL + i * 4 + c
                    part = mine * tail[i * 8 : (i + 1) * 8, c * 128 : c * 128 + n]
                    acc[t, :, :n] = acc[t, :, :n] + part if add else part

    def new_sources(k):
        r = rid[k]
        grad = dot3(rh[r], rl[r], gh[:W], gl[:W], 1, 0)
        rows, state = adagrad(x[...], xst[...], grad)
        x[...] = rows
        xst[...] = state
        xh[...], xl[...] = split(rows)

    def update(u, _):
        def send(number, src, dst, peer):
            copy = pltpu.make_async_remote_copy(
                src_ref=src,
                dst_ref=dst,
                send_sem=ssem.at[u, number],
                recv_sem=rsem.at[u, number],
                device_id=peer,
                device_id_type=MESH,
            )
            copy.start()
            return copy

        k = 2 * u
        queries(k)
        scores(k, None)
        moved = []
        for c in range(2):
            new_targets(k, c)
            moved.append(send_targets(k, c))
        query_grad()
        operator_grad(k, False)
        new_sources(k)
        queries(k + 1)
        scores(k + 1, moved)
        query_grad()
        operator_grad(k + 1, True)

        sent = [send(N_EX, acc.at[pl.ds((1 - core) * HALF, HALF)], rx.at[u], other)]
        new_sources(k + 1)
        sent[0].wait_recv()
        r1[...] = acc[pl.ds(core * HALF, HALF)] + rx[u]
        got = []
        for j in range(1, 4):
            p = (first + j) % 4
            got.append(send(N_1 + j - 1, r1.at[pl.ds(p * P1, P1)], b1.at[u, j - 1], first_peer(p)))
        sent += got
        for c in range(2):
            new_targets(k + 1, c)
        for copy in got:
            copy.wait_recv()
        moved2 = [send_targets(k + 1, c) for c in range(2)]
        r2[...] = r1[pl.ds(first * P1, P1)] + b1[u, 0] + b1[u, 1] + b1[u, 2]
        got = []
        for j in range(1, 4):
            p = (second + j) % 4
            got.append(send(N_2 + j - 1, r2.at[pl.ds(p * P2, P2)], r3.at[u, j - 1], second_peer(p)))
        sent += got
        for copy in got:
            copy.wait_recv()
        b2[:P2] = r2[pl.ds(second * P2, P2)] + r3[u, 0] + r3[u, 1] + r3[u, 2]
        got = []
        for j in range(1, NZ):
            p = (my_z + j) % NZ
            got.append(send(N_3 + j - 1, b2.at[pl.ds(p * P3, P3)], g3.at[u, j], z_peer(p)))
        sent += got
        for copy in got:
            copy.wait_recv()
        total = b2[pl.ds(my_z * P3, P3)]
        for j in range(1, NZ):
            total = total + g3[u, j]
        g3[u, 0] = gradient_scale * total
        mine = pl.ds(my_z * P3, P3)
        g2[u, mine] = g3[u, 0]
        got = []
        for j in range(1, NZ):
            p = (my_z + j) % NZ
            got.append(send(N_4 + j - 1, g3.at[u, 0], g2.at[u, mine], z_peer(p)))
        sent += got
        for copy in got:
            copy.wait_recv()
        mine = pl.ds((core * 4 + first) * P1 + second * P2, P2)
        gall[u, mine] = g2[u, pl.ds(0, P2)]
        got = []
        for j in range(1, 4):
            p = (second + j) % 4
            got.append(send(N_5 + j - 1, g2.at[u, pl.ds(0, P2)], gall.at[u, mine], second_peer(p)))
        sent += got
        for copy in got:
            copy.wait_recv()
        mine = pl.ds((core * 4 + first) * P1, P1)
        got = []
        for j in range(1, 4):
            p = (first + j) % 4
            got.append(send(N_6 + j - 1, gall.at[u, mine], gall.at[u, mine], first_peer(p)))
        sent += got
        across = [send(N_7, gall.at[u, mine], gall.at[u, mine], other)]
        for j in range(1, 4):
            got[j - 1].wait_recv()
            theirs = pl.ds((core * 4 + (first + 4 - j) % 4) * P1, P1)
            across.append(send(N_7 + j, gall.at[u, theirs], gall.at[u, theirs], other))
        sent += across
        for copy in across:
            copy.wait_recv()

        for r in range(2):
            for c in range(3):
                part = gall[u, pl.ds(r * MAIN + c * 50, 50)].reshape(W, 128)
                og_out[u, r, :, c * 128 : (c + 1) * 128] = part
            rows = []
            for i in range(2):
                t = 2 * MAIN + r * TAIL + i * 4
                rows.append(jnp.concatenate([gall[u, t + c] for c in range(4)], axis=1))
            rows.append(jnp.zeros((112, D), f32))
            tail = jnp.concatenate(rows, axis=0).T
            og_out[u, r, :, 384:] = tail[:W, :16]
            rel_new = rel[r] - operator_rate * og_out[u, r]
            rel[r] = rel_new
            rh[r], rl[r] = split(rel_new)
        for copy in moved + moved2:
            copy.wait_send()
        for copy in sent:
            copy.wait_send()
        for copy in moved2:
            copy.wait_recv()
        return 0

    lax.fori_loop(0, STEPS // 2, update, 0)
    for c in range(2):
        y_out[:, c * C : (c + 1) * C] = yin[STEPS, c, :W]
        yst_out[:, c * C : (c + 1) * C] = yin[STEPS, c, W : W + 1]


def shards(
    source_rows, source_state, target_rows, destination_state, positives, relation_ids, relations
):
    everyone = S * lax.axis_size("blk") * lax.axis_size("grp")
    gradient_scale = grad_gain / math.sqrt(everyone)
    vmem = pl.BlockSpec(memory_space=pltpu.VMEM)
    smem = pl.BlockSpec(memory_space=pltpu.SMEM)
    tiles = (8, 128)
    out = pl.pallas_call(
        functools.partial(kernel, gradient_scale),
        out_shape=(
            jax.ShapeDtypeStruct((W, S), f32),
            jax.ShapeDtypeStruct((1, S), f32),
            jax.ShapeDtypeStruct((W, D), f32),
            jax.ShapeDtypeStruct((1, D), f32),
            jax.ShapeDtypeStruct((2, W, W), f32),
            jax.ShapeDtypeStruct((2, 2, W, W), f32),
        ),
        in_specs=[vmem, vmem, vmem, vmem, vmem, smem, vmem],
        out_specs=(vmem,) * 6,
        scratch_shapes=[
            pltpu.VMEM((STEPS + 1, 2, W + 8, C), f32),
            pltpu.VMEM((STEPS, 2, W + 8, C), f32),
            pltpu.VMEM((W, S), bf16),
            pltpu.VMEM((W, S), bf16),
            pltpu.VMEM((W, D), bf16),
            pltpu.VMEM((W, D), bf16),
            pltpu.VMEM((W, S), bf16),
            pltpu.VMEM((W, S), bf16),
            pltpu.VMEM((D, S), f32),
            pltpu.VMEM((D, S), bf16),
            pltpu.VMEM((D, S), bf16),
            pltpu.VMEM((D, S), bf16),
            pltpu.VMEM((D, S), bf16),
            pltpu.VMEM((2, W, W), bf16),
            pltpu.VMEM((2, W, W), bf16),
            pltpu.VMEM((TILES, *tiles), f32),
            pltpu.VMEM((2, HALF, *tiles), f32),
            pltpu.VMEM((HALF, *tiles), f32),
            pltpu.VMEM((2, 3, P1, *tiles), f32),
            pltpu.VMEM((P1, *tiles), f32),
            pltpu.VMEM((P3 * NZ, *tiles), f32),
            pltpu.VMEM((2, 3, P2, *tiles), f32),
            pltpu.VMEM((2, NZ, P3, *tiles), f32),
            pltpu.VMEM((2, P3 * NZ, *tiles), f32),
            pltpu.VMEM((2, TILES, *tiles), f32),
            pltpu.SemaphoreType.DMA((STEPS, 2)),
            pltpu.SemaphoreType.DMA((STEPS, 2)),
            pltpu.SemaphoreType.DMA((2, N_ALL)),
            pltpu.SemaphoreType.DMA((2, N_ALL)),
        ],
        compiler_params=pltpu.CompilerParams(
            collective_id=0, has_side_effects=True, vmem_limit_bytes=58 << 20
        ),
        name="train",
    )(
        source_rows[0, 0],
        source_state[0],
        target_rows[0, 0],
        destination_state[0],
        positives[:, 0],
        relation_ids[:, 0, 0],
        relations,
    )
    source, source_state, target, target_state, relations, grads = out
    return (
        source[None, None],
        source_state[None],
        target[None, None],
        target_state[None],
        relations,
        grads,
    )


def solution(mesh):
    in_specs = (
        P("blk", "grp", None, None),
        P("blk", "grp", None),
        P("blk", "grp", None, None),
        P("blk", "grp", None),
        P(None, "blk", "grp", None),
        P(None, "blk", "grp"),
        P(),
    )
    out_specs = (
        P("blk", "grp", None, None),
        P("blk", "grp", None),
        P("blk", "grp", None, None),
        P("blk", "grp", None),
        P(),
        P(),
    )
    return jax.shard_map(shards, mesh=mesh, in_specs=in_specs, out_specs=out_specs, check_vma=False)
```

profile of v0, /device:TPU:1, one launch (start us, length us, event | category | flops | bytes accessed | tf_op | source)
XLA Modules:
  0.0 153.3 jit_solution(13343187361759035719)
XLA Ops:
  0.6 143.8 %train.1 = (f32[400,768]{1,0:T(8,128)}, f32[1,768]{1,0:T(1,128)}, f32[400,512]{1,0:T(8,128)}, f32[1,512]{1,0:T(1,128)}, f32[2,400,400]{2,1,0:T(8,128)}, /*index=5*/f32[2,2,400,400]{3,2,1,0:T(8,128)}) custom-call(f32[400,768]{1,0:T(8,128)} %bitcast.10, f32[1,768]{1,0:T(1,128)} %bitcast.15, f32[400,512]{1,0:T(8,128)} %bitcast.12, f32[1,512]{1,0:T(1,128)} %bitcast.17, ...), custom_call_target="tpu_custom_call" | custom-call | tf_op jit(solution)/shard_map/train/pallas_call | solution.py:343
  144.4 0.0 copy-start.3
  144.4 0.0 copy-start.2
  144.4 0.0 copy-start.4
  144.4 0.0 copy-start.1
  144.4 2.5 %copy.19 = f32[1,1,400,768]{3,2,1,0:T(8,128)} copy(f32[1,1,400,768]{3,2,1,0:T(8,128)} %bitcast.11) | data formatting | bytes 2457600
  147.0 0.0 copy-done.3
  147.0 0.6 copy.20
  147.6 0.0 copy-done.2
  147.6 0.9 copy.21
  148.5 0.0 copy-done.4
  148.5 0.6 copy.22
  149.0 0.0 copy-done.1
  149.1 0.0 copy-start
  149.1 1.2 copy.23
  150.2 1.4 copy-done
  151.6 1.7 %copy.24 = f32[2,2,400,400]{3,2,1,0:T(8,128)} copy(f32[2,2,400,400]{3,2,1,0:T(8,128)S(1)} %copy-done) | data formatting | bytes 5120000
Async XLA Ops:
  144.4 2.6 %copy-start.3 = (f32[1,768]{1,0:T(1,128)S(1)}, f32[1,768]{1,0:T(1,128)}, u32[]{:S(2)}) copy-start(f32[1,768]{1,0:T(1,128)} %get-tuple-element.13) | copy-start | bytes 9220
  144.4 3.2 %copy-start.2 = (f32[400,512]{1,0:T(8,128)S(1)}, f32[400,512]{1,0:T(8,128)}, u32[]{:S(2)}) copy-start(f32[400,512]{1,0:T(8,128)} %get-tuple-element.14) | copy-start | bytes 2457604
  144.4 4.0 %copy-start.4 = (f32[1,512]{1,0:T(1,128)S(1)}, f32[1,512]{1,0:T(1,128)}, u32[]{:S(2)}) copy-start(f32[1,512]{1,0:T(1,128)} %get-tuple-element.15) | copy-start | bytes 6148
  144.4 4.6 %copy-start.1 = (f32[2,400,400]{2,1,0:T(8,128)S(1)}, f32[2,400,400]{2,1,0:T(8,128)}, u32[]{:S(2)}) copy-start(f32[2,400,400]{2,1,0:T(8,128)} %get-tuple-element.28) | copy-start | bytes 3840004
  149.1 2.5 %copy-start = (f32[2,2,400,400]{3,2,1,0:T(8,128)S(1)}, f32[2,2,400,400]{3,2,1,0:T(8,128)}, u32[]{:S(2)}) copy-start(f32[2,2,400,400]{3,2,1,0:T(8,128)} %get-tuple-element.29) | copy-start | bytes 7680004
where the time goes:
time: 154 us; the launch traced here: 153 us
  Pallas kernels  144 us (94%)
  local copies, waits for them, and re-layouts  8.83 us (6%)
    pallas_call x1, Pallas kernels, shards(): pl.pallas_call(functools.partial(kernel, gradient_scale), out_shape=(jax....  144 us
    unnamed x16, local copies, waits for them, and re-layouts  8.83 us

commit v1 on v0

--- a/solution.py
+++ b/solution.py
@@ -22,8 +22,11 @@
 STEPS = 4
 NX, NY, NZ = 4, 4, 8
 MAIN, TAIL, TILES = 150, 8, 320
+PART = 100
 HALF, P1, P2, P3 = TILES // 2, TILES // 8, TILES // 32, 2
-N_EX, N_1, N_2, N_3, N_4, N_5, N_6, N_7, N_ALL = 0, 1, 4, 7, 14, 21, 24, 27, 31
+N_EX, N_1, N_2, N_3, N_4, N_5, N_6, N_7, N_ALL = 0, 2, 5, 8, 15, 22, 25, 28, 32
+RING_ORDER = (2, 1, 3)
+Z_ORDER = (4, 3, 5, 2, 6, 1, 7)
 
 
 def dot(a, b, ca, cb):
@@ -48,6 +51,18 @@
 def adagrad(values, state, gradient):
     state_new = state + jnp.sum(gradient * gradient, axis=0, keepdims=True) * (1.0 / W)
     return values - gradient * (entity_rate / jnp.sqrt(state_new)), state_new
+
+
+def unpack(gall, u, r, store):
+    base = r * HALF
+    for c in range(3):
+        store(c * 128, (c + 1) * 128, gall[u, pl.ds(base + c * 50, 50)].reshape(W, 128))
+    rows = []
+    for i in range(2):
+        t = base + MAIN + i * 4
+        rows.append(jnp.concatenate([gall[u, t + c] for c in range(4)], axis=1))
+    rows.append(jnp.zeros((112, D), f32))
+    store(384, W, jnp.concatenate(rows, axis=0).T[:W, :16])
 
 
 def kernel(
@@ -59,12 +74,13 @@
     pos,
     rid,
     rel_in,
-    x,
+    x_out,
     xst,
     y_out,
-    yst_out,
+    gall_out,
+    x,
+    y,
     rel,
-    og_out,
     yin,
     ysend,
     xh,
@@ -94,6 +110,7 @@
     y_rsem,
     ssem,
     rsem,
+    lsem,
 ):
     blk, grp = lax.axis_index("blk"), lax.axis_index("grp")
     core = blk % 2
@@ -127,20 +144,27 @@
     for peer in peers:
         pl.semaphore_signal(barrier, inc=1, device_id=peer, device_id_type=MESH)
 
-    x[...] = x_in[...]
+    loads = [
+        pltpu.make_async_copy(src, dst, lsem.at[n])
+        for n, (src, dst) in enumerate(((rel_in, rel), (x_in, x), (y_in, y)))
+    ]
+    for copy in loads:
+        copy.start()
     xst[...] = xst_in[...]
-    rel[...] = rel_in[...]
-    xh[...], xl[...] = split(x_in[...])
-    rh[...], rl[...] = split(rel_in[...])
-    for c in range(2):
-        yin[0, c, :W] = y_in[:, c * C : (c + 1) * C]
-        yin[0, c, W:] = jnp.broadcast_to(yst_in[:, c * C : (c + 1) * C], (8, C))
     gh[W:] = jnp.zeros((D - W, S), bf16)
     gl[W:] = jnp.zeros((D - W, S), bf16)
-    acc[2 * MAIN :] = jnp.zeros((TILES - 2 * MAIN, 8, 128), f32)
+    for r in range(2):
+        pad = r * HALF + MAIN
+        acc[pad : pad + 10] = jnp.zeros((10, 8, 128), f32)
     b2[P2:] = jnp.zeros((P3 * NZ - P2, 8, 128), f32)
-
-    pl.semaphore_wait(barrier, len(peers))
+    loads[0].wait()
+    rh[...], rl[...] = split(rel[...])
+    loads[1].wait()
+    xh[...], xl[...] = split(x[...])
+    loads[2].wait()
+    for c in range(2):
+        yin[0, c, :W] = y[:, c * C : (c + 1) * C]
+        yin[0, c, W:] = jnp.broadcast_to(yst_in[:, c * C : (c + 1) * C], (8, C))
 
     def queries(k):
         r = rid[k]
@@ -185,21 +209,26 @@
     def query_grad():
         gh[:W], gl[:W] = split(dot3(yh[...], yl[...], sh[...], sl[...], 1, 0))
 
-    def operator_grad(k, add):
-        og = dot3(xh[...], xl[...], gh[...], gl[...], 1, 1)
-        tail = og[:, 384:].T[:16]
+    def operator_grad(k, h, add):
+        part = slice(h * 256, (h + 1) * 256)
+        og = dot3(xh[...], xl[...], gh[part], gl[part], 1, 1)
         for r in range(2):
-            mine = (rid[k] == r).astype(f32)
-            for c in range(3):
-                at_ = pl.ds(r * MAIN + c * 50, 50)
-                part = mine * og[:, c * 128 : (c + 1) * 128].reshape(50, 8, 128)
-                acc[at_] = acc[at_] + part if add else part
+            mine = rid[k] == r
+            for c in range(2 - h):
+                to = pl.ds(r * HALF + (2 * h + c) * 50, 50)
+                new = jnp.where(mine, og[:, c * 128 : (c + 1) * 128].reshape(50, 8, 128), 0.0)
+                acc[to] = acc[to] + new if add else new
+        if h == 0:
+            return
+        tail = og[:, 128:].T[:16]
+        for r in range(2):
+            mine = rid[k] == r
             for i in range(2):
                 for c in range(4):
                     n = 128 if c < 3 else 16
-                    t = 2 * MAIN + r * TAIL + i * 4 + c
-                    part = mine * tail[i * 8 : (i + 1) * 8, c * 128 : c * 128 + n]
-                    acc[t, :, :n] = acc[t, :, :n] + part if add else part
+                    t = r * HALF + MAIN + i * 4 + c
+                    new = jnp.where(mine, tail[i * 8 : (i + 1) * 8, c * 128 : c * 128 + n], 0.0)
+                    acc[t, :, :n] = acc[t, :, :n] + new if add else new
 
     def new_sources(k):
         r = rid[k]
@@ -225,43 +254,64 @@
         k = 2 * u
         queries(k)
         scores(k, None)
-        moved = []
-        for c in range(2):
-            new_targets(k, c)
-            moved.append(send_targets(k, c))
+        new_targets(k, 0)
+
+        @pl.when(u == 0)
+        def _():
+            pl.semaphore_wait(barrier, len(peers))
+
+        moved = [send_targets(k, 0)]
+        new_targets(k, 1)
+        moved.append(send_targets(k, 1))
         query_grad()
-        operator_grad(k, False)
+        for h in range(2):
+            operator_grad(k, h, False)
         new_sources(k)
         queries(k + 1)
         scores(k + 1, moved)
         query_grad()
-        operator_grad(k + 1, True)
-
-        sent = [send(N_EX, acc.at[pl.ds((1 - core) * HALF, HALF)], rx.at[u], other)]
+
+        sent = []
+        for h in range(2):
+            operator_grad(k + 1, h, True)
+            start, size = (0, PART) if h == 0 else (PART, HALF - PART)
+            theirs = pl.ds((1 - core) * HALF + start, size)
+            sent.append(send(N_EX + h, acc.at[theirs], rx.at[u, pl.ds(start, size)], other))
         new_sources(k + 1)
-        sent[0].wait_recv()
-        r1[...] = acc[pl.ds(core * HALF, HALF)] + rx[u]
+
+        @pl.when(u == 1)
+        def _():
+            pltpu.make_async_copy(x, x_out, lsem.at[3]).start()
+
+        for copy in sent:
+            copy.wait_recv()
+
+        def chip_sum(p):
+            r1[pl.ds(p * P1, P1)] = acc[pl.ds(core * HALF + p * P1, P1)] + rx[u, pl.ds(p * P1, P1)]
+
         got = []
-        for j in range(1, 4):
+        for j in RING_ORDER:
             p = (first + j) % 4
+            chip_sum(p)
             got.append(send(N_1 + j - 1, r1.at[pl.ds(p * P1, P1)], b1.at[u, j - 1], first_peer(p)))
+        chip_sum(first)
         sent += got
         for c in range(2):
             new_targets(k + 1, c)
         for copy in got:
             copy.wait_recv()
-        moved2 = [send_targets(k + 1, c) for c in range(2)]
         r2[...] = r1[pl.ds(first * P1, P1)] + b1[u, 0] + b1[u, 1] + b1[u, 2]
         got = []
-        for j in range(1, 4):
+        for j in RING_ORDER:
             p = (second + j) % 4
             got.append(send(N_2 + j - 1, r2.at[pl.ds(p * P2, P2)], r3.at[u, j - 1], second_peer(p)))
         sent += got
+        moved2 = [send_targets(k + 1, c) for c in range(2)]
         for copy in got:
             copy.wait_recv()
         b2[:P2] = r2[pl.ds(second * P2, P2)] + r3[u, 0] + r3[u, 1] + r3[u, 2]
         got = []
-        for j in range(1, NZ):
+        for j in Z_ORDER:
             p = (my_z + j) % NZ
             got.append(send(N_3 + j - 1, b2.at[pl.ds(p * P3, P3)], g3.at[u, j], z_peer(p)))
         sent += got
@@ -274,7 +324,7 @@
         mine = pl.ds(my_z * P3, P3)
         g2[u, mine] = g3[u, 0]
         got = []
-        for j in range(1, NZ):
+        for j in Z_ORDER:
             p = (my_z + j) % NZ
             got.append(send(N_4 + j - 1, g3.at[u, 0], g2.at[u, mine], z_peer(p)))
         sent += got
@@ -283,7 +333,7 @@
         mine = pl.ds((core * 4 + first) * P1 + second * P2, P2)
         gall[u, mine] = g2[u, pl.ds(0, P2)]
         got = []
-        for j in range(1, 4):
+        for j in RING_ORDER:
             p = (second + j) % 4
             got.append(send(N_5 + j - 1, g2.at[u, pl.ds(0, P2)], gall.at[u, mine], second_peer(p)))
         sent += got
@@ -291,45 +341,64 @@
             copy.wait_recv()
         mine = pl.ds((core * 4 + first) * P1, P1)
         got = []
-        for j in range(1, 4):
+        for j in RING_ORDER:
             p = (first + j) % 4
             got.append(send(N_6 + j - 1, gall.at[u, mine], gall.at[u, mine], first_peer(p)))
         sent += got
         across = [send(N_7, gall.at[u, mine], gall.at[u, mine], other)]
-        for j in range(1, 4):
-            got[j - 1].wait_recv()
+        for n, j in ((1, 1), (2, 3), (0, 2)):
+            got[n].wait_recv()
             theirs = pl.ds((core * 4 + (first + 4 - j) % 4) * P1, P1)
             across.append(send(N_7 + j, gall.at[u, theirs], gall.at[u, theirs], other))
         sent += across
         for copy in across:
             copy.wait_recv()
 
-        for r in range(2):
-            for c in range(3):
-                part = gall[u, pl.ds(r * MAIN + c * 50, 50)].reshape(W, 128)
-                og_out[u, r, :, c * 128 : (c + 1) * 128] = part
-            rows = []
-            for i in range(2):
-                t = 2 * MAIN + r * TAIL + i * 4
-                rows.append(jnp.concatenate([gall[u, t + c] for c in range(4)], axis=1))
-            rows.append(jnp.zeros((112, D), f32))
-            tail = jnp.concatenate(rows, axis=0).T
-            og_out[u, r, :, 384:] = tail[:W, :16]
-            rel_new = rel[r] - operator_rate * og_out[u, r]
-            rel[r] = rel_new
-            rh[r], rl[r] = split(rel_new)
-        for copy in moved + moved2:
-            copy.wait_send()
-        for copy in sent:
+        @pl.when(u == 0)
+        def _():
+            for r in range(2):
+
+                def store(start, end, values):
+                    rel[r, :, start:end] = rel[r, :, start:end] - operator_rate * values
+
+                unpack(gall, u, r, store)
+                rh[r], rl[r] = split(rel[r])
+
+        for copy in moved + moved2 + sent:
             copy.wait_send()
         for copy in moved2:
             copy.wait_recv()
         return 0
 
     lax.fori_loop(0, STEPS // 2, update, 0)
+    stores = [
+        pltpu.make_async_copy(yin.at[STEPS], y_out, lsem.at[4]),
+        pltpu.make_async_copy(gall, gall_out, lsem.at[5]),
+    ]
+    for copy in stores:
+        copy.start()
+    for copy in stores:
+        copy.wait()
+    pltpu.make_async_copy(x, x_out, lsem.at[3]).wait()
+
+
+def finish(x, xst, yin, gall, rel, x_out, xst_out, y_out, yst_out, rel_out, og_out, sem):
+    copy = pltpu.make_async_copy(x, x_out, sem)
+    copy.start()
+    xst_out[...] = xst[...]
     for c in range(2):
-        y_out[:, c * C : (c + 1) * C] = yin[STEPS, c, :W]
-        yst_out[:, c * C : (c + 1) * C] = yin[STEPS, c, W : W + 1]
+        y_out[:, c * C : (c + 1) * C] = yin[c, :W]
+        yst_out[:, c * C : (c + 1) * C] = yin[c, W : W + 1]
+    for r in range(2):
+        for u in range(2):
+
+            def store(start, end, values):
+                og_out[u, r, :, start:end] = values
+                before = rel[r, :, start:end] if u == 0 else rel_out[r, :, start:end]
+                rel_out[r, :, start:end] = before - operator_rate * values
+
+            unpack(gall, u, r, store)
+    copy.wait()
 
 
 def shards(
@@ -339,20 +408,22 @@
     gradient_scale = grad_gain / math.sqrt(everyone)
     vmem = pl.BlockSpec(memory_space=pltpu.VMEM)
     smem = pl.BlockSpec(memory_space=pltpu.SMEM)
+    hbm = pl.BlockSpec(memory_space=pl.ANY)
     tiles = (8, 128)
-    out = pl.pallas_call(
+    source, source_state, target, grads = pl.pallas_call(
         functools.partial(kernel, gradient_scale),
         out_shape=(
             jax.ShapeDtypeStruct((W, S), f32),
             jax.ShapeDtypeStruct((1, S), f32),
-            jax.ShapeDtypeStruct((W, D), f32),
-            jax.ShapeDtypeStruct((1, D), f32),
-            jax.ShapeDtypeStruct((2, W, W), f32),
-            jax.ShapeDtypeStruct((2, 2, W, W), f32),
+            jax.ShapeDtypeStruct((2, W + 8, C), f32),
+            jax.ShapeDtypeStruct((2, TILES, *tiles), f32),
         ),
-        in_specs=[vmem, vmem, vmem, vmem, vmem, smem, vmem],
-        out_specs=(vmem,) * 6,
+        in_specs=[hbm, vmem, hbm, vmem, vmem, smem, hbm],
+        out_specs=(hbm, vmem, hbm, hbm),
         scratch_shapes=[
+            pltpu.VMEM((W, S), f32),
+            pltpu.VMEM((W, D), f32),
+            pltpu.VMEM((2, W, W), f32),
             pltpu.VMEM((STEPS + 1, 2, W + 8, C), f32),
             pltpu.VMEM((STEPS, 2, W + 8, C), f32),
             pltpu.VMEM((W, S), bf16),
@@ -382,9 +453,10 @@
             pltpu.SemaphoreType.DMA((STEPS, 2)),
             pltpu.SemaphoreType.DMA((2, N_ALL)),
             pltpu.SemaphoreType.DMA((2, N_ALL)),
+            pltpu.SemaphoreType.DMA((6,)),
         ],
         compiler_params=pltpu.CompilerParams(
-            collective_id=0, has_side_effects=True, vmem_limit_bytes=58 << 20
+            collective_id=0, has_side_effects=True, vmem_limit_bytes=36 << 20
         ),
         name="train",
     )(
@@ -396,6 +468,22 @@
         relation_ids[:, 0, 0],
         relations,
     )
+    out = pl.pallas_call(
+        finish,
+        out_shape=(
+            jax.ShapeDtypeStruct((W, S), f32),
+            jax.ShapeDtypeStruct((1, S), f32),
+            jax.ShapeDtypeStruct((W, D), f32),
+            jax.ShapeDtypeStruct((1, D), f32),
+            jax.ShapeDtypeStruct((2, W, W), f32),
+            jax.ShapeDtypeStruct((2, 2, W, W), f32),
+        ),
+        in_specs=[hbm, vmem, vmem, vmem, vmem],
+        out_specs=(hbm, vmem, vmem, vmem, vmem, vmem),
+        scratch_shapes=[pltpu.SemaphoreType.DMA],
+        compiler_params=pltpu.CompilerParams(vmem_limit_bytes=24 << 20),
+        name="finish",
+    )(source, source_state, target, grads, relations)
     source, source_state, target, target_state, relations, grads = out
     return (
         source[None, None],

time: 154 us -> 142 us (0.922)
  Pallas kernels: 144 us -> 134 us
  local copies, waits for them, and re-layouts: 8.83 us -> 6.58 us
    pallas_call x1, Pallas kernels: 144 us -> 130 us  [shards(): pl.pallas_call(functools.partial(kernel, gradient_scale), out_shape=(jax....]
    pallas_call x0 -> x1, Pallas kernels: none -> 3.57 us  [shards(): pl.pallas_call(finish, out_shape=(jax.ShapeDtypeStruct((W, S), f32), jax....]
    unnamed x16 -> x14, local copies, waits for them, and re-layouts: 8.83 us -> 6.58 us
where the time goes in v1:
time: 142 us; the launch traced here: 141 us
  Pallas kernels  134 us (94%)
  local copies, waits for them, and re-layouts  6.58 us (5%)
    pallas_call x1, Pallas kernels, shards(): pl.pallas_call(functools.partial(kernel, gradient_scale), out_shape=(jax....  130 us
    unnamed x14, local copies, waits for them, and re-layouts  6.58 us
    pallas_call x1, Pallas kernels, shards(): pl.pallas_call(finish, out_shape=(jax.ShapeDtypeStruct((W, S), f32), jax....  3.57 us

profile of v1, /device:TPU:1, one launch (start us, length us, event | category | flops | bytes accessed | tf_op | source)
XLA Modules:
  0.0 141.3 jit_solution(14366759824597718060)
XLA Ops:
  0.6 0.0 copy-start
  0.6 1.4 %copy-done = f32[2,400,400]{2,1,0:T(8,128)S(1)} copy-done((f32[2,400,400]{2,1,0:T(8,128)S(1)}, f32[2,400,400]{2,1,0:T(8,128)}, u32[]{:S(2)}) %copy-start) | copy-done | bytes 1280024
  2.1 0.0 copy-start.1
  2.1 1.3 copy-done.1
  3.4 0.0 copy-start.2
  3.4 1.1 copy-done.2
  4.5 0.0 copy-start.3
  4.5 0.7 copy-done.3
  5.2 0.0 copy-start.4
  5.2 0.7 copy-done.4
  5.9 0.0 copy-start.5
  5.9 0.7 copy-done.5
  6.6 0.0 copy-start.6
  6.6 0.7 copy-done.6
  7.2 130.5 %train.1 = (f32[400,768]{1,0:T(8,128)S(1)}, f32[1,768]{1,0:T(1,128)S(1)}, f32[2,408,256]{2,1,0:T(8,128)S(1)}, f32[2,320,8,128]{3,2,1,0:T(8,128)S(1)}) custom-call(f32[400,768]{1,0:T(8,128)S(1)} %bitcast.10, f32[1,768]{1,0:T(1,128)S(1)} %bitcast.13, f32[400,512]{1,0:T(8,128)S(1)} %bitcast.11, f32[1,512]{1,0:T(1,128)S(1)} %bitcast.14, ...), custom_call_target="tpu_custom_call" | custom-call | tf_op jit(solution)/shard_map/train/pallas_call | solution.py:413
  137.7 3.6 %finish.1 = (f32[400,768]{1,0:T(8,128)}, f32[1,768]{1,0:T(1,128)}, f32[400,512]{1,0:T(8,128)}, f32[1,512]{1,0:T(1,128)}, f32[2,400,400]{2,1,0:T(8,128)}, /*index=5*/f32[2,2,400,400]{3,2,1,0:T(8,128)}) custom-call(f32[400,768]{1,0:T(8,128)S(1)} %get-tuple-element.16.x, f32[1,768]{1,0:T(1,128)S(1)} %get-tuple-element.17.xst, ...), custom_call_target="tpu_custom_call" | custom-call | tf_op jit(solution)/shard_map/finish/pallas_call | solution.py:471
Async XLA Ops:
  0.6 1.4 %copy-start = (f32[2,400,400]{2,1,0:T(8,128)S(1)}, f32[2,400,400]{2,1,0:T(8,128)}, u32[]{:S(2)}) copy-start(f32[2,400,400]{2,1,0:T(8,128)} %rel.1) | copy-start | bytes 3840004
  2.1 1.3 copy-start.1
  3.4 1.1 copy-start.2
  4.5 0.7 copy-start.3
  5.2 0.7 copy-start.4
  5.9 0.7 copy-start.5
  6.6 0.7 copy-start.6

commit v2 on v1

--- a/solution.py
+++ b/solution.py
@@ -71,17 +71,18 @@
     xst_in,
     y_in,
     yst_in,
+    pos_in,
+    rid_in,
+    rel_in,
+    x,
+    xst,
+    yin,
+    gall,
+    y,
+    yst,
     pos,
     rid,
-    rel_in,
-    x_out,
-    xst,
-    y_out,
-    gall_out,
-    x,
-    y,
     rel,
-    yin,
     ysend,
     xh,
     xl,
@@ -105,7 +106,6 @@
     r3,
     g3,
     g2,
-    gall,
     y_ssem,
     y_rsem,
     ssem,
@@ -146,11 +146,20 @@
 
     loads = [
         pltpu.make_async_copy(src, dst, lsem.at[n])
-        for n, (src, dst) in enumerate(((rel_in, rel), (x_in, x), (y_in, y)))
+        for n, (src, dst) in enumerate(
+            (
+                (rel_in, rel),
+                (rid_in, rid),
+                (x_in, x),
+                (y_in, y),
+                (yst_in, yst),
+                (pos_in, pos),
+                (xst_in, xst),
+            )
+        )
     ]
     for copy in loads:
         copy.start()
-    xst[...] = xst_in[...]
     gh[W:] = jnp.zeros((D - W, S), bf16)
     gl[W:] = jnp.zeros((D - W, S), bf16)
     for r in range(2):
@@ -160,11 +169,13 @@
     loads[0].wait()
     rh[...], rl[...] = split(rel[...])
     loads[1].wait()
+    loads[2].wait()
     xh[...], xl[...] = split(x[...])
-    loads[2].wait()
+    for copy in loads[3:]:
+        copy.wait()
     for c in range(2):
         yin[0, c, :W] = y[:, c * C : (c + 1) * C]
-        yin[0, c, W:] = jnp.broadcast_to(yst_in[:, c * C : (c + 1) * C], (8, C))
+        yin[0, c, W:] = jnp.broadcast_to(yst[:, c * C : (c + 1) * C], (8, C))
 
     def queries(k):
         r = rid[k]
@@ -279,10 +290,6 @@
             sent.append(send(N_EX + h, acc.at[theirs], rx.at[u, pl.ds(start, size)], other))
         new_sources(k + 1)
 
-        @pl.when(u == 1)
-        def _():
-            pltpu.make_async_copy(x, x_out, lsem.at[3]).start()
-
         for copy in sent:
             copy.wait_recv()
 
@@ -351,19 +358,20 @@
             theirs = pl.ds((core * 4 + (first + 4 - j) % 4) * P1, P1)
             across.append(send(N_7 + j, gall.at[u, theirs], gall.at[u, theirs], other))
         sent += across
-        for copy in across:
-            copy.wait_recv()
-
-        @pl.when(u == 0)
-        def _():
-            for r in range(2):
-
-                def store(start, end, values):
-                    rel[r, :, start:end] = rel[r, :, start:end] - operator_rate * values
-
+
+        def apply(r):
+            def store(start, end, values):
+                rel[r, :, start:end] = rel[r, :, start:end] - operator_rate * values
+
+            @pl.when(u == 0)
+            def _():
                 unpack(gall, u, r, store)
                 rh[r], rl[r] = split(rel[r])
 
+        apply(core)
+        for copy in across:
+            copy.wait_recv()
+        apply(1 - core)
         for copy in moved + moved2 + sent:
             copy.wait_send()
         for copy in moved2:
@@ -371,34 +379,34 @@
         return 0
 
     lax.fori_loop(0, STEPS // 2, update, 0)
-    stores = [
-        pltpu.make_async_copy(yin.at[STEPS], y_out, lsem.at[4]),
-        pltpu.make_async_copy(gall, gall_out, lsem.at[5]),
-    ]
-    for copy in stores:
+
+
+def finish(x, xst, yin, gall, rel, x_out, xst_out, y_out, yst_out, rel_out, og_out, og, rel_new, sem):
+    copies = [pltpu.make_async_copy(x, x_out, sem.at[0])]
+    for c in range(2):
+        part = pl.ds(c * C, C)
+        rows = yin.at[STEPS, c, pl.ds(0, W)]
+        copies.append(pltpu.make_async_copy(rows, y_out.at[:, part], sem.at[1 + c]))
+    for copy in copies:
         copy.start()
-    for copy in stores:
-        copy.wait()
-    pltpu.make_async_copy(x, x_out, lsem.at[3]).wait()
-
-
-def finish(x, xst, yin, gall, rel, x_out, xst_out, y_out, yst_out, rel_out, og_out, sem):
-    copy = pltpu.make_async_copy(x, x_out, sem)
-    copy.start()
     xst_out[...] = xst[...]
     for c in range(2):
-        y_out[:, c * C : (c + 1) * C] = yin[c, :W]
-        yst_out[:, c * C : (c + 1) * C] = yin[c, W : W + 1]
+        yst_out[:, c * C : (c + 1) * C] = yin[STEPS, c, W : W + 1]
     for r in range(2):
         for u in range(2):
 
             def store(start, end, values):
-                og_out[u, r, :, start:end] = values
-                before = rel[r, :, start:end] if u == 0 else rel_out[r, :, start:end]
-                rel_out[r, :, start:end] = before - operator_rate * values
+                og[u, r, :, start:end] = values
+                before = rel[r, :, start:end] if u == 0 else rel_new[r, :, start:end]
+                rel_new[r, :, start:end] = before - operator_rate * values
 
             unpack(gall, u, r, store)
-    copy.wait()
+            copies.append(pltpu.make_async_copy(og.at[u, r], og_out.at[u, r], sem.at[3 + 2 * u + r]))
+            copies[-1].start()
+        copies.append(pltpu.make_async_copy(rel_new.at[r], rel_out.at[r], sem.at[7 + r]))
+        copies[-1].start()
+    for copy in copies:
+        copy.wait()
 
 
 def shards(
@@ -407,24 +415,33 @@
     everyone = S * lax.axis_size("blk") * lax.axis_size("grp")
     gradient_scale = grad_gain / math.sqrt(everyone)
     vmem = pl.BlockSpec(memory_space=pltpu.VMEM)
-    smem = pl.BlockSpec(memory_space=pltpu.SMEM)
-    hbm = pl.BlockSpec(memory_space=pl.ANY)
+    hbm = pl.BlockSpec(memory_space=pltpu.HBM)
     tiles = (8, 128)
+    operands = (
+        source_rows[0, 0],
+        source_state[0],
+        target_rows[0, 0],
+        destination_state[0],
+        positives[:, 0],
+        relation_ids[:, 0, 0],
+        relations,
+    )
     source, source_state, target, grads = pl.pallas_call(
         functools.partial(kernel, gradient_scale),
         out_shape=(
             jax.ShapeDtypeStruct((W, S), f32),
             jax.ShapeDtypeStruct((1, S), f32),
-            jax.ShapeDtypeStruct((2, W + 8, C), f32),
+            jax.ShapeDtypeStruct((STEPS + 1, 2, W + 8, C), f32),
             jax.ShapeDtypeStruct((2, TILES, *tiles), f32),
         ),
-        in_specs=[hbm, vmem, hbm, vmem, vmem, smem, hbm],
-        out_specs=(hbm, vmem, hbm, hbm),
+        in_specs=[hbm] * 7,
+        out_specs=(vmem,) * 4,
         scratch_shapes=[
-            pltpu.VMEM((W, S), f32),
             pltpu.VMEM((W, D), f32),
+            pltpu.VMEM((1, D), f32),
+            pltpu.VMEM((STEPS, 1, S), jnp.int32),
+            pltpu.SMEM((STEPS,), jnp.int32),
             pltpu.VMEM((2, W, W), f32),
-            pltpu.VMEM((STEPS + 1, 2, W + 8, C), f32),
             pltpu.VMEM((STEPS, 2, W + 8, C), f32),
             pltpu.VMEM((W, S), bf16),
             pltpu.VMEM((W, S), bf16),
@@ -448,26 +465,17 @@
             pltpu.VMEM((2, 3, P2, *tiles), f32),
             pltpu.VMEM((2, NZ, P3, *tiles), f32),
             pltpu.VMEM((2, P3 * NZ, *tiles), f32),
-            pltpu.VMEM((2, TILES, *tiles), f32),
             pltpu.SemaphoreType.DMA((STEPS, 2)),
             pltpu.SemaphoreType.DMA((STEPS, 2)),
             pltpu.SemaphoreType.DMA((2, N_ALL)),
             pltpu.SemaphoreType.DMA((2, N_ALL)),
-            pltpu.SemaphoreType.DMA((6,)),
+            pltpu.SemaphoreType.DMA((7,)),
         ],
         compiler_params=pltpu.CompilerParams(
             collective_id=0, has_side_effects=True, vmem_limit_bytes=36 << 20
         ),
         name="train",
-    )(
-        source_rows[0, 0],
-        source_state[0],
-        target_rows[0, 0],
-        destination_state[0],
-        positives[:, 0],
-        relation_ids[:, 0, 0],
-        relations,
-    )
+    )(*(pltpu.with_memory_space_constraint(operand, pltpu.HBM) for operand in operands))
     out = pl.pallas_call(
         finish,
         out_shape=(
@@ -478,9 +486,13 @@
             jax.ShapeDtypeStruct((2, W, W), f32),
             jax.ShapeDtypeStruct((2, 2, W, W), f32),
         ),
-        in_specs=[hbm, vmem, vmem, vmem, vmem],
-        out_specs=(hbm, vmem, vmem, vmem, vmem, vmem),
-        scratch_shapes=[pltpu.SemaphoreType.DMA],
+        in_specs=[vmem] * 5,
+        out_specs=(hbm, vmem, hbm, vmem, hbm, hbm),
+        scratch_shapes=[
+            pltpu.VMEM((2, 2, W, W), f32),
+            pltpu.VMEM((2, W, W), f32),
+            pltpu.SemaphoreType.DMA((9,)),
+        ],
         compiler_params=pltpu.CompilerParams(vmem_limit_bytes=24 << 20),
         name="finish",
     )(source, source_state, target, grads, relations)

time: 142 us -> 135 us (0.951)
  local copies, waits for them, and re-layouts: 6.58 us -> 0.01 us
    unnamed x14 -> x2, local copies, waits for them, and re-layouts: 6.58 us -> 0.01 us
where the time goes in v2:
time: 135 us
  Pallas kernels  134 us (99%)
    pallas_call x1, Pallas kernels, shards(): pl.pallas_call(functools.partial(kernel, gradient_scale), out_shape=(jax....  131 us
    pallas_call x1, Pallas kernels, shards(): pl.pallas_call(finish, out_shape=(jax.ShapeDtypeStruct((W, S), f32), jax....  3.53 us

profile of v2, /device:TPU:1, one launch (start us, length us, event | category | flops | bytes accessed | tf_op | source)
XLA Modules:
  0.0 134.7 jit_solution(18185955745473228024)
XLA Ops:
  0.6 0.0 copy-start
  0.6 130.5 %train.1 = (f32[400,768]{1,0:T(8,128)S(1)}, f32[1,768]{1,0:T(1,128)S(1)}, f32[5,2,408,256]{3,2,1,0:T(8,128)S(1)}, f32[2,320,8,128]{3,2,1,0:T(8,128)S(1)}) custom-call(f32[400,768]{1,0:T(8,128)} %bitcast.10, f32[1,768]{1,0:T(1,128)} %bitcast.13, f32[400,512]{1,0:T(8,128)} %bitcast.11, f32[1,512]{1,0:T(1,128)} %bitcast.14, s32[4,1,768]{2,1,0:T(1,128)} %bitcast.12, ...), custom_call_target="tpu_custom_call" | custom-call | tf_op jit(solution)/shard_map/train/pallas_call | solution.py:429
  131.2 0.0 copy-done
  131.2 3.5 %finish.1 = (f32[400,768]{1,0:T(8,128)}, f32[1,768]{1,0:T(1,128)}, f32[400,512]{1,0:T(8,128)}, f32[1,512]{1,0:T(1,128)}, f32[2,400,400]{2,1,0:T(8,128)}, /*index=5*/f32[2,2,400,400]{3,2,1,0:T(8,128)}) custom-call(f32[400,768]{1,0:T(8,128)S(1)} %get-tuple-element.16.x, f32[1,768]{1,0:T(1,128)S(1)} %get-tuple-element.17.xst, ...), custom_call_target="tpu_custom_call" | custom-call | tf_op jit(solution)/shard_map/finish/pallas_call | solution.py:479
Async XLA Ops:
  0.6 130.5 %copy-start = (f32[2,400,400]{2,1,0:T(8,128)S(1)}, f32[2,400,400]{2,1,0:T(8,128)}, u32[]{:S(2)}) copy-start(f32[2,400,400]{2,1,0:T(8,128)} %rel.1) | copy-start | bytes 3840004

commit v3 on v2

--- a/solution.py
+++ b/solution.py
@@ -24,8 +24,9 @@
 MAIN, TAIL, TILES = 150, 8, 320
 PART = 100
 HALF, P1, P2, P3 = TILES // 2, TILES // 8, TILES // 32, 2
-N_EX, N_1, N_2, N_3, N_4, N_5, N_6, N_7, N_ALL = 0, 2, 5, 8, 15, 22, 25, 28, 32
+N_EX, N_1, N_2, N_3, N_4, N_5, N_6, N_7, N_ALL = 0, 2, 14, 17, 24, 31, 34, 46, 62
 RING_ORDER = (2, 1, 3)
+ARRIVAL = (1, 3, 2)
 Z_ORDER = (4, 3, 5, 2, 6, 1, 7)
 
 
@@ -296,32 +297,41 @@
         def chip_sum(p):
             r1[pl.ds(p * P1, P1)] = acc[pl.ds(core * HALF + p * P1, P1)] + rx[u, pl.ds(p * P1, P1)]
 
-        got = []
-        for j in RING_ORDER:
-            p = (first + j) % 4
+        for p in range(4):
             chip_sum(p)
-            got.append(send(N_1 + j - 1, r1.at[pl.ds(p * P1, P1)], b1.at[u, j - 1], first_peer(p)))
-        chip_sum(first)
-        sent += got
+        got = {}
+        for t in (*RING_ORDER, 0):
+            q = (second + t) % 4
+            for j in RING_ORDER:
+                p = (first + j) % 4
+                src = r1.at[pl.ds(p * P1 + q * P2, P2)]
+                n = 4 * (j - 1) + t
+                got[j, t] = send(N_1 + n, src, b1.at[u, n], first_peer(p))
+        sent += got.values()
         for c in range(2):
             new_targets(k + 1, c)
-        for copy in got:
+
+        def ring_sum(t):
+            for j in ARRIVAL:
+                got[j, t].wait_recv()
+            own = r1[pl.ds(first * P1 + (second + t) % 4 * P2, P2)]
+            return own + b1[u, t] + b1[u, 4 + t] + b1[u, 8 + t]
+
+        got2 = []
+        for t in RING_ORDER:
+            r2[t] = ring_sum(t)
+            got2.append(send(N_2 + t - 1, r2.at[t], r3.at[u, t - 1], second_peer((second + t) % 4)))
+        sent += got2
+        total = ring_sum(0)
+        for copy in got2:
             copy.wait_recv()
-        r2[...] = r1[pl.ds(first * P1, P1)] + b1[u, 0] + b1[u, 1] + b1[u, 2]
-        got = []
-        for j in RING_ORDER:
-            p = (second + j) % 4
-            got.append(send(N_2 + j - 1, r2.at[pl.ds(p * P2, P2)], r3.at[u, j - 1], second_peer(p)))
-        sent += got
-        moved2 = [send_targets(k + 1, c) for c in range(2)]
-        for copy in got:
-            copy.wait_recv()
-        b2[:P2] = r2[pl.ds(second * P2, P2)] + r3[u, 0] + r3[u, 1] + r3[u, 2]
+        b2[:P2] = total + r3[u, 0] + r3[u, 1] + r3[u, 2]
         got = []
         for j in Z_ORDER:
             p = (my_z + j) % NZ
             got.append(send(N_3 + j - 1, b2.at[pl.ds(p * P3, P3)], g3.at[u, j], z_peer(p)))
         sent += got
+        moved2 = [send_targets(k + 1, c) for c in range(2)]
         for copy in got:
             copy.wait_recv()
         total = b2[pl.ds(my_z * P3, P3)]
@@ -337,27 +347,38 @@
         sent += got
         for copy in got:
             copy.wait_recv()
-        mine = pl.ds((core * 4 + first) * P1 + second * P2, P2)
+        def place(f, s_):
+            return pl.ds((core * 4 + f) * P1 + s_ * P2, P2)
+
+        across, around = [], {}
+
+        def cross(n, where):
+            across.append(send(N_7 + n, gall.at[u, where], gall.at[u, where], other))
+
+        def spread(t, where):
+            for j in RING_ORDER:
+                n = 4 * (j - 1) + t
+                peer = first_peer((first + j) % 4)
+                around[j, t] = send(N_6 + n, gall.at[u, where], gall.at[u, where], peer)
+
+        mine = place(first, second)
         gall[u, mine] = g2[u, pl.ds(0, P2)]
-        got = []
+        got2 = {}
         for j in RING_ORDER:
-            p = (second + j) % 4
-            got.append(send(N_5 + j - 1, g2.at[u, pl.ds(0, P2)], gall.at[u, mine], second_peer(p)))
-        sent += got
-        for copy in got:
-            copy.wait_recv()
-        mine = pl.ds((core * 4 + first) * P1, P1)
-        got = []
-        for j in RING_ORDER:
-            p = (first + j) % 4
-            got.append(send(N_6 + j - 1, gall.at[u, mine], gall.at[u, mine], first_peer(p)))
-        sent += got
-        across = [send(N_7, gall.at[u, mine], gall.at[u, mine], other)]
-        for n, j in ((1, 1), (2, 3), (0, 2)):
-            got[n].wait_recv()
-            theirs = pl.ds((core * 4 + (first + 4 - j) % 4) * P1, P1)
-            across.append(send(N_7 + j, gall.at[u, theirs], gall.at[u, theirs], other))
-        sent += across
+            peer = second_peer((second + j) % 4)
+            got2[j] = send(N_5 + j - 1, gall.at[u, mine], gall.at[u, mine], peer)
+        spread(0, mine)
+        cross(0, mine)
+        for t in ARRIVAL:
+            got2[t].wait_recv()
+            theirs = place(first, (second + 4 - t) % 4)
+            spread(t, theirs)
+            cross(t, theirs)
+        for t in (0, *ARRIVAL):
+            for j in ARRIVAL:
+                around[j, t].wait_recv()
+                cross(4 * j + t, place((first + 4 - j) % 4, (second + 4 - t) % 4))
+        sent += [*got2.values(), *around.values(), *across]
 
         def apply(r):
             def store(start, end, values):
@@ -459,8 +480,8 @@
             pltpu.VMEM((TILES, *tiles), f32),
             pltpu.VMEM((2, HALF, *tiles), f32),
             pltpu.VMEM((HALF, *tiles), f32),
-            pltpu.VMEM((2, 3, P1, *tiles), f32),
-            pltpu.VMEM((P1, *tiles), f32),
+            pltpu.VMEM((2, 12, P2, *tiles), f32),
+            pltpu.VMEM((4, P2, *tiles), f32),
             pltpu.VMEM((P3 * NZ, *tiles), f32),
             pltpu.VMEM((2, 3, P2, *tiles), f32),
             pltpu.VMEM((2, NZ, P3, *tiles), f32),

time: 135 us -> 133 us (0.985); the launches traced: 135 us -> 131 us
  Pallas kernels: 134 us -> 130 us
    pallas_call x1, Pallas kernels: 131 us -> 126 us  [shards(): pl.pallas_call(functools.partial(kernel, gradient_scale), out_shape=(jax....]
where the time goes in v3:
time: 133 us; the launch traced here: 131 us
  Pallas kernels  130 us (98%)
    pallas_call x1, Pallas kernels, shards(): pl.pallas_call(functools.partial(kernel, gradient_scale), out_shape=(jax....  126 us
    pallas_call x1, Pallas kernels, shards(): pl.pallas_call(finish, out_shape=(jax.ShapeDtypeStruct((W, S), f32), jax....  3.53 us

profile of v3, /device:TPU:1, one launch (start us, length us, event | category | flops | bytes accessed | tf_op | source)
XLA Modules:
  0.0 130.5 jit_solution(7710141474094116407)
XLA Ops:
  0.6 0.0 copy-start
  0.6 126.3 %train.1 = (f32[400,768]{1,0:T(8,128)S(1)}, f32[1,768]{1,0:T(1,128)S(1)}, f32[5,2,408,256]{3,2,1,0:T(8,128)S(1)}, f32[2,320,8,128]{3,2,1,0:T(8,128)S(1)}) custom-call(f32[400,768]{1,0:T(8,128)} %bitcast.10, f32[1,768]{1,0:T(1,128)} %bitcast.13, f32[400,512]{1,0:T(8,128)} %bitcast.11, f32[1,512]{1,0:T(1,128)} %bitcast.14, s32[4,1,768]{2,1,0:T(1,128)} %bitcast.12, ...), custom_call_target="tpu_custom_call" | custom-call | tf_op jit(solution)/shard_map/train/pallas_call | solution.py:450
  127.0 0.0 copy-done
  127.0 3.5 %finish.1 = (f32[400,768]{1,0:T(8,128)}, f32[1,768]{1,0:T(1,128)}, f32[400,512]{1,0:T(8,128)}, f32[1,512]{1,0:T(1,128)}, f32[2,400,400]{2,1,0:T(8,128)}, /*index=5*/f32[2,2,400,400]{3,2,1,0:T(8,128)}) custom-call(f32[400,768]{1,0:T(8,128)S(1)} %get-tuple-element.16.x, f32[1,768]{1,0:T(1,128)S(1)} %get-tuple-element.17.xst, ...), custom_call_target="tpu_custom_call" | custom-call | tf_op jit(solution)/shard_map/finish/pallas_call | solution.py:500
Async XLA Ops:
  0.6 126.3 %copy-start = (f32[2,400,400]{2,1,0:T(8,128)S(1)}, f32[2,400,400]{2,1,0:T(8,128)}, u32[]{:S(2)}) copy-start(f32[2,400,400]{2,1,0:T(8,128)} %rel.1) | copy-start | bytes 3840004

commit v4 on v3

--- a/solution.py
+++ b/solution.py
@@ -281,6 +281,10 @@
         new_sources(k)
         queries(k + 1)
         scores(k + 1, moved)
+        moved2 = []
+        for c in range(2):
+            new_targets(k + 1, c)
+            moved2.append(send_targets(k + 1, c))
         query_grad()
 
         sent = []
@@ -308,9 +312,6 @@
                 n = 4 * (j - 1) + t
                 got[j, t] = send(N_1 + n, src, b1.at[u, n], first_peer(p))
         sent += got.values()
-        for c in range(2):
-            new_targets(k + 1, c)
-
         def ring_sum(t):
             for j in ARRIVAL:
                 got[j, t].wait_recv()
@@ -331,7 +332,6 @@
             p = (my_z + j) % NZ
             got.append(send(N_3 + j - 1, b2.at[pl.ds(p * P3, P3)], g3.at[u, j], z_peer(p)))
         sent += got
-        moved2 = [send_targets(k + 1, c) for c in range(2)]
         for copy in got:
             copy.wait_recv()
         total = b2[pl.ds(my_z * P3, P3)]

time: 133 us -> 127 us (0.955); the launches traced: 131 us -> 127 us
  Pallas kernels: 130 us -> 126 us
    pallas_call x1, Pallas kernels: 126 us -> 123 us  [shards(): pl.pallas_call(functools.partial(kernel, gradient_scale), out_shape=(jax....]
where the time goes in v4:
time: 127 us
  Pallas kernels  126 us (99%)
    pallas_call x1, Pallas kernels, shards(): pl.pallas_call(functools.partial(kernel, gradient_scale), out_shape=(jax....  123 us
    pallas_call x1, Pallas kernels, shards(): pl.pallas_call(finish, out_shape=(jax.ShapeDtypeStruct((W, S), f32), jax....  3.53 us

profile of v4, /device:TPU:1, one launch (start us, length us, event | category | flops | bytes accessed | tf_op | source)
XLA Modules:
  0.0 126.8 jit_solution(122260698200941349)
XLA Ops:
  0.6 0.0 copy-start
  0.6 122.6 %train.1 = (f32[400,768]{1,0:T(8,128)S(1)}, f32[1,768]{1,0:T(1,128)S(1)}, f32[5,2,408,256]{3,2,1,0:T(8,128)S(1)}, f32[2,320,8,128]{3,2,1,0:T(8,128)S(1)}) custom-call(f32[400,768]{1,0:T(8,128)} %bitcast.10, f32[1,768]{1,0:T(1,128)} %bitcast.13, f32[400,512]{1,0:T(8,128)} %bitcast.11, f32[1,512]{1,0:T(1,128)} %bitcast.14, s32[4,1,768]{2,1,0:T(1,128)} %bitcast.12, ...), custom_call_target="tpu_custom_call" | custom-call | tf_op jit(solution)/shard_map/train/pallas_call | solution.py:450
  123.3 0.0 copy-done
  123.3 3.5 %finish.1 = (f32[400,768]{1,0:T(8,128)}, f32[1,768]{1,0:T(1,128)}, f32[400,512]{1,0:T(8,128)}, f32[1,512]{1,0:T(1,128)}, f32[2,400,400]{2,1,0:T(8,128)}, /*index=5*/f32[2,2,400,400]{3,2,1,0:T(8,128)}) custom-call(f32[400,768]{1,0:T(8,128)S(1)} %get-tuple-element.16.x, f32[1,768]{1,0:T(1,128)S(1)} %get-tuple-element.17.xst, ...), custom_call_target="tpu_custom_call" | custom-call | tf_op jit(solution)/shard_map/finish/pallas_call | solution.py:500
Async XLA Ops:
  0.6 122.6 %copy-start = (f32[2,400,400]{2,1,0:T(8,128)S(1)}, f32[2,400,400]{2,1,0:T(8,128)}, u32[]{:S(2)}) copy-start(f32[2,400,400]{2,1,0:T(8,128)} %rel.1) | copy-start | bytes 3840004

commit v5 on v3

--- a/solution.py
+++ b/solution.py
@@ -206,8 +206,8 @@
         ysend[k, c, :W] = rows
         ysend[k, c, W:] = jnp.broadcast_to(state, (8, C))
 
-    def send_targets(k, c):
-        copy = pltpu.make_async_remote_copy(
+    def target_copy(k, c):
+        return pltpu.make_async_remote_copy(
             src_ref=ysend.at[k, c],
             dst_ref=yin.at[k + 1, c],
             send_sem=y_ssem.at[k, c],
@@ -215,6 +215,9 @@
             device_id=behind,
             device_id_type=MESH,
         )
+
+    def send_targets(k, c):
+        copy = target_copy(k, c)
         copy.start()
         return copy
 
@@ -281,6 +284,16 @@
         new_sources(k)
         queries(k + 1)
         scores(k + 1, moved)
+
+        def targets_of(which):
+            @pl.when(core == which)
+            def _():
+                for c in range(2):
+                    new_targets(k + 1, c)
+                    send_targets(k + 1, c)
+
+        targets_of(1)
+        moved2 = [target_copy(k + 1, c) for c in range(2)]
         query_grad()
 
         sent = []
@@ -289,8 +302,6 @@
             start, size = (0, PART) if h == 0 else (PART, HALF - PART)
             theirs = pl.ds((1 - core) * HALF + start, size)
             sent.append(send(N_EX + h, acc.at[theirs], rx.at[u, pl.ds(start, size)], other))
-        new_sources(k + 1)
-
         for copy in sent:
             copy.wait_recv()
 
@@ -308,8 +319,8 @@
                 n = 4 * (j - 1) + t
                 got[j, t] = send(N_1 + n, src, b1.at[u, n], first_peer(p))
         sent += got.values()
-        for c in range(2):
-            new_targets(k + 1, c)
+        targets_of(0)
+        new_sources(k + 1)
 
         def ring_sum(t):
             for j in ARRIVAL:
@@ -331,7 +342,6 @@
             p = (my_z + j) % NZ
             got.append(send(N_3 + j - 1, b2.at[pl.ds(p * P3, P3)], g3.at[u, j], z_peer(p)))
         sent += got
-        moved2 = [send_targets(k + 1, c) for c in range(2)]
         for copy in got:
             copy.wait_recv()
         total = b2[pl.ds(my_z * P3, P3)]

time: 133 us -> 123 us (0.925); the launches traced: 131 us -> 123 us
  Pallas kernels: 130 us -> 122 us
    pallas_call x1, Pallas kernels: 126 us -> 118 us  [shards(): pl.pallas_call(functools.partial(kernel, gradient_scale), out_shape=(jax....]
where the time goes in v5:
time: 123 us
  Pallas kernels  122 us (99%)
    pallas_call x1, Pallas kernels, shards(): pl.pallas_call(functools.partial(kernel, gradient_scale), out_shape=(jax....  118 us
    pallas_call x1, Pallas kernels, shards(): pl.pallas_call(finish, out_shape=(jax.ShapeDtypeStruct((W, S), f32), jax....  3.53 us

profile of v5, /device:TPU:1, one launch (start us, length us, event | category | flops | bytes accessed | tf_op | source)
XLA Modules:
  0.0 122.6 jit_solution(18000302673921828758)
XLA Ops:
  0.6 0.0 copy-start
  0.6 118.4 %train.1 = (f32[400,768]{1,0:T(8,128)S(1)}, f32[1,768]{1,0:T(1,128)S(1)}, f32[5,2,408,256]{3,2,1,0:T(8,128)S(1)}, f32[2,320,8,128]{3,2,1,0:T(8,128)S(1)}) custom-call(f32[400,768]{1,0:T(8,128)} %bitcast.10, f32[1,768]{1,0:T(1,128)} %bitcast.13, f32[400,512]{1,0:T(8,128)} %bitcast.11, f32[1,512]{1,0:T(1,128)} %bitcast.14, s32[4,1,768]{2,1,0:T(1,128)} %bitcast.12, ...), custom_call_target="tpu_custom_call" | custom-call | tf_op jit(solution)/shard_map/train/pallas_call | solution.py:460
  119.1 0.0 copy-done
  119.1 3.5 %finish.1 = (f32[400,768]{1,0:T(8,128)}, f32[1,768]{1,0:T(1,128)}, f32[400,512]{1,0:T(8,128)}, f32[1,512]{1,0:T(1,128)}, f32[2,400,400]{2,1,0:T(8,128)}, /*index=5*/f32[2,2,400,400]{3,2,1,0:T(8,128)}) custom-call(f32[400,768]{1,0:T(8,128)S(1)} %get-tuple-element.16.x, f32[1,768]{1,0:T(1,128)S(1)} %get-tuple-element.17.xst, ...), custom_call_target="tpu_custom_call" | custom-call | tf_op jit(solution)/shard_map/finish/pallas_call | solution.py:510
Async XLA Ops:
  0.6 118.5 %copy-start = (f32[2,400,400]{2,1,0:T(8,128)S(1)}, f32[2,400,400]{2,1,0:T(8,128)}, u32[]{:S(2)}) copy-start(f32[2,400,400]{2,1,0:T(8,128)} %rel.1) | copy-start | bytes 3840004

commit v6 on v5

--- a/solution.py
+++ b/solution.py
@@ -302,13 +302,13 @@
             start, size = (0, PART) if h == 0 else (PART, HALF - PART)
             theirs = pl.ds((1 - core) * HALF + start, size)
             sent.append(send(N_EX + h, acc.at[theirs], rx.at[u, pl.ds(start, size)], other))
-        for copy in sent:
-            copy.wait_recv()
 
         def chip_sum(p):
             r1[pl.ds(p * P1, P1)] = acc[pl.ds(core * HALF + p * P1, P1)] + rx[u, pl.ds(p * P1, P1)]
 
         for p in range(4):
+            if p % 2 == 0:
+                sent[p // 2].wait_recv()
             chip_sum(p)
         got = {}
         for t in (*RING_ORDER, 0):

time: 123 us -> 123 us (level)
  no operation moved by 1% of the time
where the time goes in v6:
time: 123 us
  Pallas kernels  122 us (99%)
    pallas_call x1, Pallas kernels, shards(): pl.pallas_call(functools.partial(kernel, gradient_scale), out_shape=(jax....  118 us
    pallas_call x1, Pallas kernels, shards(): pl.pallas_call(finish, out_shape=(jax.ShapeDtypeStruct((W, S), f32), jax....  3.53 us

profile of v6, /device:TPU:1, one launch (start us, length us, event | category | flops | bytes accessed | tf_op | source)
XLA Modules:
  0.0 122.7 jit_solution(5853724409864806026)
XLA Ops:
  0.6 0.0 copy-start
  0.6 118.5 %train.1 = (f32[400,768]{1,0:T(8,128)S(1)}, f32[1,768]{1,0:T(1,128)S(1)}, f32[5,2,408,256]{3,2,1,0:T(8,128)S(1)}, f32[2,320,8,128]{3,2,1,0:T(8,128)S(1)}) custom-call(f32[400,768]{1,0:T(8,128)} %bitcast.10, f32[1,768]{1,0:T(1,128)} %bitcast.13, f32[400,512]{1,0:T(8,128)} %bitcast.11, f32[1,512]{1,0:T(1,128)} %bitcast.14, s32[4,1,768]{2,1,0:T(1,128)} %bitcast.12, ...), custom_call_target="tpu_custom_call" | custom-call | tf_op jit(solution)/shard_map/train/pallas_call | solution.py:460
  119.1 0.0 copy-done
  119.1 3.5 %finish.1 = (f32[400,768]{1,0:T(8,128)}, f32[1,768]{1,0:T(1,128)}, f32[400,512]{1,0:T(8,128)}, f32[1,512]{1,0:T(1,128)}, f32[2,400,400]{2,1,0:T(8,128)}, /*index=5*/f32[2,2,400,400]{3,2,1,0:T(8,128)}) custom-call(f32[400,768]{1,0:T(8,128)S(1)} %get-tuple-element.16.x, f32[1,768]{1,0:T(1,128)S(1)} %get-tuple-element.17.xst, ...), custom_call_target="tpu_custom_call" | custom-call | tf_op jit(solution)/shard_map/finish/pallas_call | solution.py:510
Async XLA Ops:
  0.6 118.5 %copy-start = (f32[2,400,400]{2,1,0:T(8,128)S(1)}, f32[2,400,400]{2,1,0:T(8,128)}, u32[]{:S(2)}) copy-start(f32[2,400,400]{2,1,0:T(8,128)} %rel.1) | copy-start | bytes 3840004
